TPU v7x, 32 devices: a whole 2x2x4 slice. The times are simulated.
32 devices in a mesh: dap: 8 (over y, x, core), dp: 4 (over z).
Axes of the slice: x: 2, y: 2, z: 4, core: 2. Of those that a mesh axis runs over, the one named last changes fastest.
Arguments:
- pair: bfloat16 [64, 16, 128], P(('dp', 'dap')), parts along dimension 0, may hold values from -6 to 6
- pair_mask: int32 [64, 16], P(('dp', 'dap')), parts along dimension 0, may hold values from 0 to 1, as said below
- w_left: bfloat16 [128, 256], replicated, may hold values from -0.5 to 0.5
- w_right: bfloat16 [128, 256], replicated, may hold values from -0.5 to 0.5
- w_tri_gate: bfloat16 [128, 128], replicated, may hold values from -0.5 to 0.5
- w_tri_out: bfloat16 [128, 128], replicated, may hold values from -0.5 to 0.5
- w_attend: bfloat16 [128, 512], replicated, may hold values from -0.5 to 0.5
- w_bias: bfloat16 [128, 4], replicated
- w_att_out: bfloat16 [128, 128], replicated, may hold values from -0.5 to 0.5
Outputs:
- pair_out: float32 [64, 16, 128], P('dp', 'dap'), parts along dimension 0
There are 4 independent parts, one for each index of `dp`. A program takes and returns all parts, laid end to end along the dimension named above; an argument that names none is the same for every part. Nothing has to cross between parts.
Inputs may be any that keep to these rules, and one draw needn't show every extreme that they name: pair_mask[i, i] = 1 for every residue i.
All inputs are finite; a program needn't handle non-finite values.
Results may differ from a plain program's by a relative error of at most 0.014.
The roundings to bfloat16 on the way count: a program that leaves them out, or rounds other values in their place, can miss the bound.
Values may be sent and summed in bfloat16 or wider, within the bound.
No kernel may reach another device: no remote copies, remote signals or barrier semaphores. Data moves between devices by JAX's collectives and lax.ppermute only.
A program may use at most 128 MiB of HBM per device.

v0:
```python
import jax
import jax.numpy as jnp
from jax import lax
from jax.sharding import PartitionSpec as P


def layer_norm(x):
    x = x.astype(jnp.float32)
    mean = jnp.mean(x, axis=-1, keepdims=True)
    var = jnp.mean((x - mean) * (x - mean), axis=-1, keepdims=True)
    return (x - mean) / jnp.sqrt(var + 1e-05)


def matmul(x, w):
    flat = x.reshape(-1, x.shape[-1])
    return jnp.dot(flat, w, preferred_element_type=jnp.float32).reshape(
        x.shape[:-1] + (w.shape[1],)
    )


def edges(zn, weight, maskf, hidden):
    both = matmul(zn, weight)
    return (jax.nn.sigmoid(both[..., :hidden]) * both[..., hidden:] * maskf[..., None]).astype(
        jnp.bfloat16
    )


def triangle_update(pair_part, zn_part, tri, w_tri_gate, w_tri_out):
    tn = layer_norm(tri).astype(jnp.bfloat16)
    update = jax.nn.sigmoid(matmul(zn_part, w_tri_gate)) * matmul(tn, w_tri_out)
    return pair_part.astype(jnp.float32) + update


def attention(pair1, mask_cols, w_attend, w_bias, w_att_out):
    inner = w_att_out.shape[0]
    heads = w_bias.shape[1]
    head_dim = inner // heads
    total, local = (pair1.shape[0], pair1.shape[1])
    yn = layer_norm(pair1).astype(jnp.bfloat16)
    proj = matmul(yn, w_attend)
    query = proj[..., :inner].astype(jnp.bfloat16).reshape(total, local, heads, head_dim)
    keys = proj[..., inner : 2 * inner].astype(jnp.bfloat16).reshape(total, local, heads, head_dim)
    values = (
        proj[..., 2 * inner : 3 * inner].astype(jnp.bfloat16).reshape(total, local, heads, head_dim)
    )
    gate = jax.nn.sigmoid(proj[..., 3 * inner :])
    bias_part = jnp.einsum("kic,ch->hki", yn, w_bias, preferred_element_type=jnp.float32).astype(
        jnp.bfloat16
    )
    bias = lax.all_gather(bias_part, "dap", axis=2, tiled=True)
    scores = jnp.einsum(
        "irhd,krhd->rhki", query, keys, preferred_element_type=jnp.float32
    ) / jnp.sqrt(jnp.float32(head_dim))
    scores = scores + bias.astype(jnp.float32)[None]
    live = jnp.transpose(mask_cols.astype(jnp.float32))[:, None, :, None]
    scores = jnp.where(live > 0.5, scores, jnp.float32(-1000000000.0))
    weights = jax.nn.softmax(scores, axis=2).astype(jnp.bfloat16)
    summed = jnp.einsum(
        "rhki,krhd->irhd", weights, values, preferred_element_type=jnp.float32
    ).reshape(total, local, inner)
    att = (gate * summed).astype(jnp.bfloat16)
    return pair1 + matmul(att, w_att_out)


def shards(pair, pair_mask, w_left, w_right, w_tri_gate, w_tri_out, w_attend, w_bias, w_att_out):
    hidden = w_tri_out.shape[0]
    maskf = pair_mask.astype(jnp.float32)
    zn = layer_norm(pair).astype(jnp.bfloat16)
    left_edge = edges(zn, w_left, maskf, hidden)
    right_edge = edges(zn, w_right, maskf, hidden)
    pair_cols, mask_cols = (
        lax.all_to_all(pair, "dap", split_axis=1, concat_axis=0, tiled=True),
        lax.all_to_all(
            pair_mask.astype(jnp.bfloat16), "dap", split_axis=1, concat_axis=0, tiled=True
        ),
    )
    tri = jnp.einsum(
        "ikc,jkc->ijc",
        lax.all_gather(left_edge, "dap", axis=0, tiled=True),
        right_edge,
        preferred_element_type=jnp.float32,
    )
    zn_cols = layer_norm(pair_cols).astype(jnp.bfloat16)
    pair1 = triangle_update(pair_cols, zn_cols, tri, w_tri_gate, w_tri_out)
    return attention(pair1, mask_cols, w_attend, w_bias, w_att_out)


def solution(mesh):
    placed = (
        P(("dp", "dap"), None, None),
        P(("dp", "dap"), None),
        P(),
        P(),
        P(),
        P(),
        P(),
        P(),
        P(),
    )
    return jax.shard_map(
        shards, mesh=mesh, in_specs=placed, out_specs=P("dp", "dap", None), check_vma=False
    )
```

profile of v0, /device:TPU:0, one launch (start us, length us, event | category | flops | bytes accessed | tf_op | source)
XLA Modules:
  0.0 41.4 jit_solution(9851496634011292177)
XLA Ops:
  0.0 0.8 %fusion.56 = (bf16[2,16]{1,0:T(2,128)(2,1)S(1)}, f32[2,16]{1,0:T(2,128)S(1)}) fusion(s32[2,16]{1,0:T(2,128)} %param.10), kind=kLoop, calls=%fused_computation.85 | loop fusion | flops 64 | bytes 320 | tf_op jit(solution)/shard_map/convert_element_type | solution.py:74
  0.8 0.6 %copy.53 = bf16[2,8,2]{2,0,1:T(2,128)(2,1)} copy(bf16[2,8,2]{2,1,0:T(8,128)(2,1)S(1)} %all_to_all.8) | data formatting | bytes 128 | tf_op jit(solution)/shard_map/all_to_all | solution.py:73
  1.5 5.2 %all-to-all-start.1 = ((bf16[2,8,2]{2,0,1:T(2,128)(2,1)}), bf16[2,8,2]{2,0,1:T(2,128)(2,1)S(1)}, u32[]{:S(2)}, u32[]{:S(2)}) async-start(bf16[2,8,2]{2,0,1:T(2,128)(2,1)} %copy.53), calls=%async_computation.1 | async-start | bytes 8192 | tf_op jit(solution)/shard_map/all_to_all | solution.py:73
  6.7 0.2 fusion.25
  6.9 1.1 %fusion.12 = f32[2,16,256]{2,1,0:T(8,128)S(1)} fusion(bf16[128,256]{1,0:T(8,128)(2,1)} %param.11, bf16[2,16,128]{2,1,0:T(8,128)(2,1)S(1)} %copy-done.1, f32[2,16]{1,0:T(2,128)S(1)} %add_sqrt_fusion.3, f32[2,16]{1,0:T(2,128)S(1)} %broadcast_multiply_fusion.3), kind=kOutput, calls=%fused_computation.18 | convolution fusion | flops 2113536 | bytes 106752 | tf_op jit(solution)/shard_map/dot_general | solution.py:16
  8.0 0.2 fusion.14
  8.3 9.7 %all_gather.6 = bf16[16,16,128]{2,1,0:T(8,128)(2,1)S(1)} all-gather(bf16[2,16,128]{2,1,0:T(8,128)(2,1)S(1)} %get-tuple-element.10), channel_id=1, replica_groups=mesh['dap'=8,'dp'=4] {'dap'}, dimensions={0}, use_global_device_ids=true | all-gather | bytes 73728 | tf_op jit(solution)/shard_map/all_gather | solution.py:79
  18.0 0.4 %copy.51 = bf16[16,16,128]{1,0,2:T(8,128)(2,1)S(1)} copy(bf16[16,16,128]{2,1,0:T(8,128)(2,1)S(1)} %all_gather.6) | data formatting | bytes 131072 | tf_op jit(solution)/shard_map/all_gather | solution.py:79
  18.6 0.4 fusion.60
  19.1 0.2 multiply_reduce_fusion.1
  19.3 0.6 %copy.48 = bf16[2,16,128]{2,0,1:T(2,128)(2,1)} copy(bf16[2,16,128]{2,1,0:T(8,128)(2,1)S(1)} %copy-done.1) | data formatting | bytes 16384 | tf_op args[0]
  19.9 3.3 %all-to-all-start = ((bf16[2,16,128]{2,0,1:T(2,128)(2,1)}), bf16[2,16,128]{2,0,1:T(2,128)(2,1)S(1)}, u32[]{:S(2)}, u32[]{:S(2)}) async-start(bf16[2,16,128]{2,0,1:T(2,128)(2,1)} %copy.48), calls=%async_computation | async-start | bytes 16384 | tf_op jit(solution)/shard_map/all_to_all | solution.py:72
  23.4 4.5 %all-to-all-done = bf16[2,16,128]{2,0,1:T(2,128)(2,1)S(1)} async-done(((bf16[2,16,128]{2,0,1:T(2,128)(2,1)}), bf16[2,16,128]{2,0,1:T(2,128)(2,1)S(1)}, u32[]{:S(2)}, u32[]{:S(2)}) %all-to-all-start) | async-done | bytes 8224 | tf_op jit(solution)/shard_map/all_to_all | solution.py:72
  28.0 0.2 fusion.42
  28.4 0.6 %copy-done.5 = bf16[128,128]{1,0:T(8,128)(2,1)S(1)} copy-done((bf16[128,128]{1,0:T(8,128)(2,1)S(1)}, bf16[128,128]{1,0:T(8,128)(2,1)}, u32[]{:S(2)}) %copy-start.5) | copy-done | bytes 32792
  29.0 0.2 fusion.8
  29.2 0.6 %copy-done.6 = bf16[128,128]{1,0:T(8,128)(2,1)S(1)} copy-done((bf16[128,128]{1,0:T(8,128)(2,1)S(1)}, bf16[128,128]{1,0:T(8,128)(2,1)}, u32[]{:S(2)}) %copy-start.6) | copy-done | bytes 32792
  29.7 0.3 fusion.57
  30.0 0.2 multiply_reduce_fusion
  30.6 0.6 %copy-done.3 = bf16[128,4]{0,1:T(4,128)(2,1)S(1)} copy-done((bf16[128,4]{0,1:T(4,128)(2,1)S(1)}, bf16[128,4]{0,1:T(4,128)(2,1)}, u32[]{:S(2)}) %copy-start.3) | copy-done | bytes 1048
  31.3 8.0 %all_gather.7 = bf16[4,16,16]{1,0,2:T(4,128)(2,1)S(1)} all-gather(bf16[4,16,2]{1,0,2:T(4,128)(2,1)S(1)} %fusion.9), channel_id=1, replica_groups=mesh['dap'=8,'dp'=4] {'dap'}, dimensions={2}, use_global_device_ids=true | all-gather | bytes 2304 | tf_op jit(solution)/shard_map/all_gather | solution.py:50
  39.7 0.2 convolution_bitcast_fusion
  40.0 0.7 %copy-done.2 = bf16[128,128]{1,0:T(8,128)(2,1)S(1)} copy-done((bf16[128,128]{1,0:T(8,128)(2,1)S(1)}, bf16[128,128]{1,0:T(8,128)(2,1)}, u32[]{:S(2)}) %copy-start.2) | copy-done | bytes 32792
  40.8 0.6 %copy.61 = f32[16,2,128]{2,1,0:T(2,128)} copy(f32[16,2,128]{2,0,1:T(8,128)S(1)} %convolution_add_fusion) | data formatting | bytes 32768 | tf_op jit(solution)/shard_map/add | solution.py:62
  (47 shorter events, 2.2 us)
Async XLA Ops:
  0.0 30.3 %copy-start = (bf16[128,512]{1,0:T(8,128)(2,1)S(1)}, bf16[128,512]{1,0:T(8,128)(2,1)}, u32[]{:S(2)}) copy-start(bf16[128,512]{1,0:T(8,128)(2,1)} %param.15) | copy-start | bytes 393220
  0.8 5.8 %copy-start.1 = (bf16[2,16,128]{2,1,0:T(8,128)(2,1)S(1)}, bf16[2,16,128]{2,1,0:T(8,128)(2,1)}, u32[]{:S(2)}) copy-start(bf16[2,16,128]{2,1,0:T(8,128)(2,1)} %param.9) | copy-start | bytes 24580
  1.5 18.5 %all-to-all-start.1 = ((bf16[2,8,2]{2,0,1:T(2,128)(2,1)}), bf16[2,8,2]{2,0,1:T(2,128)(2,1)S(1)}, u32[]{:S(2)}, u32[]{:S(2)}) async-start(bf16[2,8,2]{2,0,1:T(2,128)(2,1)} %copy.53), calls=%async_computation.1 | async-start | bytes 8192 | tf_op jit(solution)/shard_map/all_to_all | solution.py:73
  6.9 1.1 %copy-start.4 = (bf16[128,256]{1,0:T(8,128)(2,1)S(1)}, bf16[128,256]{1,0:T(8,128)(2,1)}, u32[]{:S(2)}) copy-start(bf16[128,256]{1,0:T(8,128)(2,1)} %param.12) | copy-start | bytes 196612
  19.9 8.0 %all-to-all-start = ((bf16[2,16,128]{2,0,1:T(2,128)(2,1)}), bf16[2,16,128]{2,0,1:T(2,128)(2,1)S(1)}, u32[]{:S(2)}, u32[]{:S(2)}) async-start(bf16[2,16,128]{2,0,1:T(2,128)(2,1)} %copy.48), calls=%async_computation | async-start | bytes 16384 | tf_op jit(solution)/shard_map/all_to_all | solution.py:72
  28.2 0.8 %copy-start.5 = (bf16[128,128]{1,0:T(8,128)(2,1)S(1)}, bf16[128,128]{1,0:T(8,128)(2,1)}, u32[]{:S(2)}) copy-start(bf16[128,128]{1,0:T(8,128)(2,1)} %param.13) | copy-start | bytes 98308
  29.0 0.8 %copy-start.6 = (bf16[128,128]{1,0:T(8,128)(2,1)S(1)}, bf16[128,128]{1,0:T(8,128)(2,1)}, u32[]{:S(2)}) copy-start(bf16[128,128]{1,0:T(8,128)(2,1)} %param.14) | copy-start | bytes 98308
  30.5 0.7 %copy-start.3 = (bf16[128,4]{0,1:T(4,128)(2,1)S(1)}, bf16[128,4]{0,1:T(4,128)(2,1)}, u32[]{:S(2)}) copy-start(bf16[128,4]{0,1:T(4,128)(2,1)} %param.16) | copy-start | bytes 3076
  39.9 0.8 %copy-start.2 = (bf16[128,128]{1,0:T(8,128)(2,1)S(1)}, bf16[128,128]{1,0:T(8,128)(2,1)}, u32[]{:S(2)}) copy-start(bf16[128,128]{1,0:T(8,128)(2,1)} %param.17) | copy-start | bytes 98308
where the time goes:
time: 42 us; the launch traced here: 41.4 us
  blocking collectives  17.7 us (42%)
  starting transfers between devices  8.53 us (20%)
  local copies, waits for them, and re-layouts  5.7 us (14%)
  waiting for transfers between devices  4.51 us (11%)
  matrix products  2.83 us (7%)
  other arithmetic  1.97 us (5%)
    all_gather x1, blocking collectives, shards(): lax.all_gather(left_edge, 'dap', axis=0, tiled=True)  9.75 us
    all_gather x1, blocking collectives, attention(): bias = lax.all_gather(bias_part, 'dap', axis=2, tiled=True)  7.98 us
    all_to_all x1, starting transfers between devices, shards(): lax.all_to_all(pair_mask.astype(jnp.bfloat16), 'dap', split_axis=1, conca...  5.2 us
    all_to_all x1, waiting for transfers between devices, shards(): lax.all_to_all(pair, 'dap', split_axis=1, concat_axis=0, tiled=True)  4.51 us
    all_to_all x1, starting transfers between devices, shards(): lax.all_to_all(pair, 'dap', split_axis=1, concat_axis=0, tiled=True)  3.33 us
    unnamed x15, local copies, waits for them, and re-layouts  3 us
    dot_general x6, matrix products, matmul(): jnp.dot(flat, w, preferred_element_type=jnp.float32)  1.99 us
  transfers between devices with their start and end apart: 2, of which 1 were waited for; matrix products, arithmetic and copies ran while one was open for 9% of the time, Pallas kernels for 0%

commit v1 on v0

--- a/solution.py
+++ b/solution.py
@@ -2,6 +2,12 @@
 import jax.numpy as jnp
 from jax import lax
 from jax.sharding import PartitionSpec as P
+
+
+def stacked_exchange(block, mesh_axis, split, join):
+    pieces = jnp.split(block, lax.axis_size(mesh_axis), axis=split)
+    received = lax.all_to_all(jnp.stack(pieces), mesh_axis, 0, 0)
+    return jnp.concatenate(received, axis=join)
 
 
 def layer_norm(x):
@@ -70,9 +76,7 @@
     right_edge = edges(zn, w_right, maskf, hidden)
     pair_cols, mask_cols = (
         lax.all_to_all(pair, "dap", split_axis=1, concat_axis=0, tiled=True),
-        lax.all_to_all(
-            pair_mask.astype(jnp.bfloat16), "dap", split_axis=1, concat_axis=0, tiled=True
-        ),
+        stacked_exchange(pair_mask.astype(jnp.bfloat16), "dap", 1, 0),
     )
     tri = jnp.einsum(
         "ikc,jkc->ijc",

time: 42 us -> 46.1 us (1.098)
  local copies, waits for them, and re-layouts: 5.7 us -> 10.1 us
    unnamed x15 -> x22, local copies, waits for them, and re-layouts: 3 us -> 7.27 us
    another operation x0 -> x1, local copies, waits for them, and re-layouts: none -> 0.59 us  [stacked_exchange(): received = lax.all_to_all(jnp.stack(pieces), mesh_axis, 0, 0)]
    all_to_all x2 -> x1, local copies, waits for them, and re-layouts: 0.69 us -> 0.1 us  [stacked_exchange(): received = lax.all_to_all(jnp.stack(pieces), mesh_axis, 0, 0)]
  transfers between devices with their start and end apart: 2 -> 2, of which waited for: 1 -> 1; matrix products, arithmetic and copies ran while one was open for 9% -> 8% of each run, Pallas kernels for 0% -> 0%
where the time goes in v1:
time: 46.1 us; the launch traced here: 45.6 us
  blocking collectives  17.7 us (38%)
  local copies, waits for them, and re-layouts  10.1 us (22%)
  starting transfers between devices  8.53 us (19%)
  waiting for transfers between devices  4.34 us (9%)
  matrix products  2.83 us (6%)
  other arithmetic  1.97 us (4%)
    all_gather x1, blocking collectives, shards(): lax.all_gather(left_edge, 'dap', axis=0, tiled=True)  9.75 us
    all_gather x1, blocking collectives, attention(): bias = lax.all_gather(bias_part, 'dap', axis=2, tiled=True)  7.98 us
    unnamed x22, local copies, waits for them, and re-layouts  7.27 us
    all_to_all x1, starting transfers between devices, stacked_exchange(): received = lax.all_to_all(jnp.stack(pieces), mesh_axis, 0, 0)  5.2 us
    all_to_all x1, waiting for transfers between devices, shards(): lax.all_to_all(pair, 'dap', split_axis=1, concat_axis=0, tiled=True)  4.34 us
    all_to_all x1, starting transfers between devices, shards(): lax.all_to_all(pair, 'dap', split_axis=1, concat_axis=0, tiled=True)  3.33 us
    dot_general x6, matrix products, matmul(): jnp.dot(flat, w, preferred_element_type=jnp.float32)  1.99 us
  transfers between devices with their start and end apart: 2, of which 1 were waited for; matrix products, arithmetic and copies ran while one was open for 8% of the time, Pallas kernels for 0%

profile of v1, /device:TPU:0, one launch (start us, length us, event | category | flops | bytes accessed | tf_op | source)
XLA Modules:
  0.0 45.6 jit_solution(15004590528022742447)
XLA Ops:
  0.0 0.8 %fusion.56 = (bf16[2,16]{1,0:T(2,128)(2,1)S(1)}, f32[2,16]{1,0:T(2,128)S(1)}) fusion(s32[2,16]{1,0:T(2,128)} %param.10), kind=kLoop, calls=%fused_computation.93 | loop fusion | flops 64 | bytes 320 | tf_op jit(solution)/shard_map/convert_element_type | solution.py:79
  0.8 0.6 %constant_dynamic-update-slice_fusion.7 = bf16[8,2,2]{2,1,0:T(2,128)(2,1)} fusion(bf16[2,16]{1,0:T(2,128)(2,1)S(1)} %get-tuple-element.8), kind=kLoop, calls=%fused_computation.41 | loop fusion | bytes 520
  1.4 0.6 %constant_dynamic-update-slice_fusion.6 = bf16[8,2,2]{2,1,0:T(2,128)(2,1)} fusion(bf16[8,2,2]{2,1,0:T(2,128)(2,1)} %constant_dynamic-update-slice_fusion.7, bf16[2,16]{1,0:T(2,128)(2,1)S(1)} %get-tuple-element.8), kind=kLoop, calls=%fused_computation.40 | loop fusion | bytes 520
  1.9 0.6 %constant_dynamic-update-slice_fusion.5 = bf16[8,2,2]{2,1,0:T(2,128)(2,1)} fusion(bf16[8,2,2]{2,1,0:T(2,128)(2,1)} %constant_dynamic-update-slice_fusion.6, bf16[2,16]{1,0:T(2,128)(2,1)S(1)} %get-tuple-element.8), kind=kLoop, calls=%fused_computation.39 | loop fusion | bytes 520
  2.5 0.7 %constant_dynamic-update-slice_fusion.4 = bf16[8,2,2]{2,1,0:T(2,128)(2,1)} fusion(bf16[8,2,2]{2,1,0:T(2,128)(2,1)} %constant_dynamic-update-slice_fusion.5, bf16[2,16]{1,0:T(2,128)(2,1)S(1)} %get-tuple-element.8), kind=kLoop, calls=%fused_computation.38 | loop fusion | bytes 520
  3.2 0.6 %constant_dynamic-update-slice_fusion.3 = bf16[8,2,2]{2,1,0:T(2,128)(2,1)} fusion(bf16[8,2,2]{2,1,0:T(2,128)(2,1)} %constant_dynamic-update-slice_fusion.4, bf16[2,16]{1,0:T(2,128)(2,1)S(1)} %get-tuple-element.8), kind=kLoop, calls=%fused_computation.37 | loop fusion | bytes 520
  3.8 0.6 %constant_dynamic-update-slice_fusion.2 = bf16[8,2,2]{2,1,0:T(2,128)(2,1)} fusion(bf16[8,2,2]{2,1,0:T(2,128)(2,1)} %constant_dynamic-update-slice_fusion.3, bf16[2,16]{1,0:T(2,128)(2,1)S(1)} %get-tuple-element.8), kind=kLoop, calls=%fused_computation.36 | loop fusion | bytes 520
  4.4 0.6 %constant_dynamic-update-slice_fusion.1 = bf16[8,2,2]{2,1,0:T(2,128)(2,1)} fusion(bf16[8,2,2]{2,1,0:T(2,128)(2,1)} %constant_dynamic-update-slice_fusion.2, bf16[2,16]{1,0:T(2,128)(2,1)S(1)} %get-tuple-element.8), kind=kLoop, calls=%fused_computation.35 | loop fusion | bytes 520
  5.0 0.6 %constant_dynamic-update-slice_fusion = bf16[8,2,2]{2,1,0:T(2,128)(2,1)} fusion(bf16[8,2,2]{2,1,0:T(2,128)(2,1)} %constant_dynamic-update-slice_fusion.1, bf16[2,16]{1,0:T(2,128)(2,1)S(1)} %get-tuple-element.8), kind=kLoop, calls=%fused_computation.34 | loop fusion | bytes 520 | tf_op jit(solution)/shard_map/stack | solution.py:9
  5.6 5.2 %all-to-all-start.1 = ((bf16[8,2,2]{2,1,0:T(2,128)(2,1)}), bf16[8,2,2]{2,1,0:T(2,128)(2,1)S(1)}, u32[]{:S(2)}, u32[]{:S(2)}) async-start(bf16[8,2,2]{2,1,0:T(2,128)(2,1)} %constant_dynamic-update-slice_fusion), calls=%async_computation.1 | async-start | bytes 8192 | tf_op jit(solution)/shard_map/all_to_all | solution.py:9
  11.1 1.1 %fusion.12 = f32[2,16,256]{2,1,0:T(8,128)S(1)} fusion(bf16[128,256]{1,0:T(8,128)(2,1)} %param.11, bf16[2,16,128]{2,1,0:T(8,128)(2,1)S(1)} %copy-done.1, f32[2,16]{1,0:T(2,128)S(1)} %add_sqrt_fusion.3, f32[2,16]{1,0:T(2,128)S(1)} %broadcast_multiply_fusion.3), kind=kOutput, calls=%fused_computation.18 | convolution fusion | flops 2113536 | bytes 106752 | tf_op jit(solution)/shard_map/dot_general | solution.py:22
  12.5 9.7 %all_gather.6 = bf16[16,16,128]{2,1,0:T(8,128)(2,1)S(1)} all-gather(bf16[2,16,128]{2,1,0:T(8,128)(2,1)S(1)} %get-tuple-element.10), channel_id=1, replica_groups=mesh['dap'=8,'dp'=4] {'dap'}, dimensions={0}, use_global_device_ids=true | all-gather | bytes 73728 | tf_op jit(solution)/shard_map/all_gather | solution.py:83
  22.2 0.4 copy.93
  22.8 0.4 fusion.60
  23.5 0.6 %copy.90 = bf16[2,16,128]{2,0,1:T(2,128)(2,1)} copy(bf16[2,16,128]{2,1,0:T(8,128)(2,1)S(1)} %copy-done.1) | data formatting | bytes 16384 | tf_op args[0]
  24.1 3.3 %all-to-all-start = ((bf16[2,16,128]{2,0,1:T(2,128)(2,1)}), bf16[2,16,128]{2,0,1:T(2,128)(2,1)S(1)}, u32[]{:S(2)}, u32[]{:S(2)}) async-start(bf16[2,16,128]{2,0,1:T(2,128)(2,1)} %copy.90), calls=%async_computation | async-start | bytes 16384 | tf_op jit(solution)/shard_map/all_to_all | solution.py:78
  27.8 4.3 %all-to-all-done = bf16[2,16,128]{2,0,1:T(2,128)(2,1)S(1)} async-done(((bf16[2,16,128]{2,0,1:T(2,128)(2,1)}), bf16[2,16,128]{2,0,1:T(2,128)(2,1)S(1)}, u32[]{:S(2)}, u32[]{:S(2)}) %all-to-all-start) | async-done | bytes 8224 | tf_op jit(solution)/shard_map/all_to_all | solution.py:78
  32.6 0.6 %copy-done.5 = bf16[128,128]{1,0:T(8,128)(2,1)S(1)} copy-done((bf16[128,128]{1,0:T(8,128)(2,1)S(1)}, bf16[128,128]{1,0:T(8,128)(2,1)}, u32[]{:S(2)}) %copy-start.5) | copy-done | bytes 32792
  33.3 0.6 %copy-done.6 = bf16[128,128]{1,0:T(8,128)(2,1)S(1)} copy-done((bf16[128,128]{1,0:T(8,128)(2,1)S(1)}, bf16[128,128]{1,0:T(8,128)(2,1)}, u32[]{:S(2)}) %copy-start.6) | copy-done | bytes 32792
  33.9 0.3 fusion.57
  34.8 0.6 %copy-done.3 = bf16[128,4]{0,1:T(4,128)(2,1)S(1)} copy-done((bf16[128,4]{0,1:T(4,128)(2,1)S(1)}, bf16[128,4]{0,1:T(4,128)(2,1)}, u32[]{:S(2)}) %copy-start.3) | copy-done | bytes 1048
  35.5 8.0 %all_gather.7 = bf16[4,16,16]{1,0,2:T(4,128)(2,1)S(1)} all-gather(bf16[4,16,2]{1,0,2:T(4,128)(2,1)S(1)} %fusion.9), channel_id=1, replica_groups=mesh['dap'=8,'dp'=4] {'dap'}, dimensions={2}, use_global_device_ids=true | all-gather | bytes 2304 | tf_op jit(solution)/shard_map/all_gather | solution.py:56
  44.2 0.7 %copy-done.2 = bf16[128,128]{1,0:T(8,128)(2,1)S(1)} copy-done((bf16[128,128]{1,0:T(8,128)(2,1)S(1)}, bf16[128,128]{1,0:T(8,128)(2,1)}, u32[]{:S(2)}) %copy-start.2) | copy-done | bytes 32792
  45.0 0.6 %copy.103 = f32[16,2,128]{2,1,0:T(2,128)} copy(f32[16,2,128]{2,0,1:T(8,128)S(1)} %convolution_add_fusion) | data formatting | bytes 32768 | tf_op jit(solution)/shard_map/add | solution.py:68
  (54 shorter events, 3.5 us)
Async XLA Ops:
  0.0 34.5 %copy-start = (bf16[128,512]{1,0:T(8,128)(2,1)S(1)}, bf16[128,512]{1,0:T(8,128)(2,1)}, u32[]{:S(2)}) copy-start(bf16[128,512]{1,0:T(8,128)(2,1)} %param.15) | copy-start | bytes 393220
  3.2 7.7 %copy-start.1 = (bf16[2,16,128]{2,1,0:T(8,128)(2,1)S(1)}, bf16[2,16,128]{2,1,0:T(8,128)(2,1)}, u32[]{:S(2)}) copy-start(bf16[2,16,128]{2,1,0:T(8,128)(2,1)} %param.9) | copy-start | bytes 24580
  5.6 18.5 %all-to-all-start.1 = ((bf16[8,2,2]{2,1,0:T(2,128)(2,1)}), bf16[8,2,2]{2,1,0:T(2,128)(2,1)S(1)}, u32[]{:S(2)}, u32[]{:S(2)}) async-start(bf16[8,2,2]{2,1,0:T(2,128)(2,1)} %constant_dynamic-update-slice_fusion), calls=%async_computation.1 | async-start | bytes 8192 | tf_op jit(solution)/shard_map/all_to_all | solution.py:9
  11.1 1.1 %copy-start.4 = (bf16[128,256]{1,0:T(8,128)(2,1)S(1)}, bf16[128,256]{1,0:T(8,128)(2,1)}, u32[]{:S(2)}) copy-start(bf16[128,256]{1,0:T(8,128)(2,1)} %param.12) | copy-start | bytes 196612
  24.1 8.0 %all-to-all-start = ((bf16[2,16,128]{2,0,1:T(2,128)(2,1)}), bf16[2,16,128]{2,0,1:T(2,128)(2,1)S(1)}, u32[]{:S(2)}, u32[]{:S(2)}) async-start(bf16[2,16,128]{2,0,1:T(2,128)(2,1)} %copy.90), calls=%async_computation | async-start | bytes 16384 | tf_op jit(solution)/shard_map/all_to_all | solution.py:78
  32.4 0.8 %copy-start.5 = (bf16[128,128]{1,0:T(8,128)(2,1)S(1)}, bf16[128,128]{1,0:T(8,128)(2,1)}, u32[]{:S(2)}) copy-start(bf16[128,128]{1,0:T(8,128)(2,1)} %param.13) | copy-start | bytes 98308
  33.1 0.8 %copy-start.6 = (bf16[128,128]{1,0:T(8,128)(2,1)S(1)}, bf16[128,128]{1,0:T(8,128)(2,1)}, u32[]{:S(2)}) copy-start(bf16[128,128]{1,0:T(8,128)(2,1)} %param.14) | copy-start | bytes 98308
  34.7 0.7 %copy-start.3 = (bf16[128,4]{0,1:T(4,128)(2,1)S(1)}, bf16[128,4]{0,1:T(4,128)(2,1)}, u32[]{:S(2)}) copy-start(bf16[128,4]{0,1:T(4,128)(2,1)} %param.16) | copy-start | bytes 3076
  44.1 0.8 %copy-start.2 = (bf16[128,128]{1,0:T(8,128)(2,1)S(1)}, bf16[128,128]{1,0:T(8,128)(2,1)}, u32[]{:S(2)}) copy-start(bf16[128,128]{1,0:T(8,128)(2,1)} %param.17) | copy-start | bytes 98308
